TPU v7x, 32 devices: a whole 2x2x4 slice. The times are simulated.
32 devices in a mesh: grp: 2 (over y), seq: 16 (over z, x, core).
Axes of the slice: x: 2, y: 2, z: 4, core: 2. Of those that a mesh axis runs over, the one named last changes fastest.
Arguments:
- inputs: bfloat16 [4, 2048, 1536], P('grp', 'seq'), parts along dimension 0, may hold values from -36 to 36
- gain: float32 [1536], replicated, may hold values from 0.1 to 1.9
- conv_weight: bfloat16 [3, 1536, 768], P(None, 'seq'), may hold values from -0.09375 to 0.09375
- proj_weight: bfloat16 [768, 1536], P(None, 'seq'), may hold values from -0.21875 to 0.21875
- head_weight: bfloat16 [1536, 512], P(None, 'seq'), may hold values from -0.15625 to 0.15625
- track_head_bias: bfloat16 [1, 512], P(None, 'seq'), may hold values from -4 to 4
- counts: int32 [4, 2048, 512], P('grp', 'seq'), parts along dimension 0, may hold values from 0 to 32
Outputs:
- input_grad: bfloat16 [4, 2048, 1536], P('grp', 'seq'), parts along dimension 0
- loss_value: float32 [2], P('grp'), parts along dimension 0
There are 2 independent parts, one for each index of `grp`. A program takes and returns all parts, laid end to end along the dimension named above; an argument that names none is the same for every part. Nothing has to cross between parts.
All inputs are finite; a program needn't handle non-finite values.
Results may differ from a plain program's by a relative error of at most 0.011.
Values may be sent and summed in bfloat16 or wider, within the bound.
A program may use at most 128 MiB of HBM per device.

v0:
```python
import jax
import jax.numpy as jnp
from jax import lax
from jax.sharding import PartitionSpec as P

SPAN = 8


def shifted(value, axis, steps):
    count = lax.axis_size(axis)
    initial, last = (max(0, -steps), min(count, count - steps))
    return lax.ppermute(value, axis, [(source, source + steps) for source in range(initial, last)])


def norm_rows(value_entries, gain):
    scale_inv = lax.rsqrt(jnp.mean(value_entries * value_entries, axis=-1, keepdims=True) + 1e-06)
    return value_entries * scale_inv * gain


def head_block(stream, head_full, bias_full, observed):
    logits = jnp.dot(stream, head_full, preferred_element_type=jnp.float32) + bias_full.astype(
        jnp.float32
    )
    poisson_rate = jax.nn.softplus(logits) + 0.05
    observed_f = observed.astype(jnp.float32)
    loss_total = jnp.sum(poisson_rate - observed_f * jnp.log(poisson_rate))
    logit_grad = ((1.0 - observed_f / poisson_rate) * jax.nn.sigmoid(logits)).astype(jnp.bfloat16)
    residual_gradient = lax.dot_general(
        logit_grad, head_full, (((1,), (1,)), ((), ())), preferred_element_type=jnp.float32
    )
    return (loss_total, residual_gradient)


def back_dot(left, right):
    return lax.dot_general(
        left, right, (((1,), (1,)), ((), ())), preferred_element_type=jnp.float32
    )


def shards(inputs, gain, conv_weight, proj_weight, head_weight, track_head_bias, counts):
    seq_count, row_count, window_width = inputs.shape
    flat_rows = seq_count * row_count
    track_count = counts.shape[2]
    conv_full, proj_full = (
        lax.all_gather(conv_weight, "seq", axis=1, tiled=True),
        lax.all_gather(proj_weight, "seq", axis=1, tiled=True),
    )
    inner = conv_full.shape[2]
    inputs_f = inputs.astype(jnp.float32)
    normed = norm_rows(inputs_f, gain).astype(jnp.bfloat16)
    normed_flat = normed.reshape(flat_rows, window_width)
    behind_rows = shifted(normed, "seq", SPAN).reshape(flat_rows, window_width)
    ahead_rows = shifted(normed, "seq", -SPAN).reshape(flat_rows, window_width)
    conv_pre = jnp.dot(normed_flat, conv_full[1], preferred_element_type=jnp.float32)
    conv_pre = conv_pre + jnp.dot(behind_rows, conv_full[0], preferred_element_type=jnp.float32)
    conv_pre = conv_pre + jnp.dot(ahead_rows, conv_full[2], preferred_element_type=jnp.float32)
    conv_act = jax.nn.gelu(conv_pre).astype(jnp.bfloat16)
    stream = (
        inputs_f.reshape(flat_rows, window_width)
        + jnp.dot(conv_act, proj_full, preferred_element_type=jnp.float32)
    ).astype(jnp.bfloat16)
    counts_flat = counts.reshape(flat_rows, track_count)
    head_full, bias_full = (
        lax.all_gather(head_weight, "seq", axis=1, tiled=True),
        lax.all_gather(track_head_bias, "seq", axis=1, tiled=True),
    )
    loss_total, residual_gradient = head_block(stream, head_full, bias_full, counts_flat)
    summed_loss = lax.psum(loss_total, "seq")
    loss_value = (summed_loss / (flat_rows * lax.axis_size("seq") * track_count)).reshape(1)
    act_grad = back_dot(residual_gradient.astype(jnp.bfloat16), proj_full)
    _, gelu_back = jax.vjp(jax.nn.gelu, conv_pre)
    pre_grad = gelu_back(act_grad)[0].astype(jnp.bfloat16)
    pre_three = pre_grad.reshape(seq_count, row_count, inner)
    grad_ahead = shifted(pre_three, "seq", -SPAN).reshape(flat_rows, inner)
    grad_behind = shifted(pre_three, "seq", SPAN).reshape(flat_rows, inner)
    normed_grad = back_dot(pre_grad, conv_full[1])
    normed_grad = normed_grad + back_dot(grad_ahead, conv_full[0])
    normed_grad = normed_grad + back_dot(grad_behind, conv_full[2])
    _, norm_back = jax.vjp(lambda value_entries: norm_rows(value_entries, gain), inputs_f)
    input_grad = (
        residual_gradient.reshape(seq_count, row_count, window_width)
        + norm_back(normed_grad.reshape(seq_count, row_count, window_width))[0]
    ).astype(jnp.bfloat16)
    return (input_grad, loss_value)


def solution(mesh):
    placed = (
        P("grp", "seq", None),
        P(),
        P(None, "seq", None),
        P(None, "seq"),
        P(None, "seq"),
        P(None, "seq"),
        P("grp", "seq", None),
    )
    return jax.shard_map(
        shards,
        mesh=mesh,
        in_specs=placed,
        out_specs=(P("grp", "seq", None), P("grp")),
        check_vma=False,
    )
```

profile of v0, /device:TPU:0, one launch (start us, length us, event | category | flops | bytes accessed | tf_op | source)
XLA Modules:
  0.0 252.3 jit_solution(4451681180811085461)
XLA Ops:
  7.2 0.0 copy-start.5
  7.2 0.0 copy-start
  7.2 0.0 copy-start.4
  7.2 0.0 all-gather.4.cloned.1.call-start
  7.2 0.7 all-gather.4.cloned.1.call-update
  7.9 0.0 all-gather.8.cloned.1.call-start
  8.0 0.7 all-gather.8.cloned.1.call-update
  8.7 0.0 all-gather.6.cloned.1.call-start
  8.7 0.7 all-gather.6.cloned.1.call-update
  9.4 1.4 multiply_reduce_fusion.1
  10.8 0.0 copy-done
  10.8 0.9 multiply_convert_fusion
  11.7 6.0 %collective-permute-start = (bf16[2,128,1536]{2,1,0:T(8,128)(2,1)S(1)}, bf16[2,128,1536]{2,1,0:T(8,128)(2,1)S(1)}, u32[]{:S(2)}, u32[]{:S(2)}) collective-permute-start(bf16[2,128,1536]{2,1,0:T(8,128)(2,1)S(1)} %multiply_convert_fusion), channel_id=1, source_target_pairs={{0,8},{1,9},{2,10},{3,11},{4,12},{5,13},{6,14},{7,15},{16,24},{17,... | collective-permute-start | bytes 2359304 | tf_op jit(solution)/shard_map/ppermute | solution.py:12
  17.8 1.3 collective-permute-start.1
  19.1 0.0 copy-done.5
  19.1 0.6 dynamic-slice
  20.3 0.0 copy-done.4
  20.4 0.2 dynamic-update-slice
  20.6 50.1 %all-reduce = bf16[512]{0:T(512)(128)(2,1)S(1)} all-reduce(bf16[512]{0:T(512)(128)(2,1)S(1)} %dynamic-update-slice), channel_id=1, replica_groups=mesh['grp'=2,'seq'=16] {'seq'}, use_global_device_ids=true, to_apply=%add | all-reduce | flops 512 | bytes 2048
  70.7 31.3 %all-gather.4.cloned.1.call-done = bf16[3,1536,768]{2,1,0:T(8,128)(2,1)} async-done(((bf16[3,96,768]{2,1,0:T(8,128)(2,1)}), bf16[3,1536,768]{2,1,0:T(8,128)(2,1)}) %all-gather.4.cloned.1.call-update) | async-done | bytes 7077904 | tf_op jit(solution)/shard_map/all_gather | solution.py:45
  101.9 2.4 fusion.2
  104.4 0.0 collective-permute-done
  104.4 2.4 fusion.8
  106.8 0.0 collective-permute-done.1
  106.8 0.0 copy-start.3
  106.8 2.5 fusion.7
  109.4 0.0 copy-start.6
  109.4 33.0 %all-gather.8.cloned.1.call-done = bf16[1536,512]{0,1:T(8,128)(2,1)} async-done(((bf16[1536,32]{0,1:T(8,128)(2,1)}), bf16[1536,512]{0,1:T(8,128)(2,1)}) %all-gather.8.cloned.1.call-update) | async-done | bytes 1572880 | tf_op jit(solution)/shard_map/all_gather | solution.py:64
  142.3 43.3 %all-gather.6.cloned.1.call-done = bf16[768,1536]{0,1:T(8,128)(2,1)} async-done(((bf16[768,96]{0,1:T(8,128)(2,1)}), bf16[768,1536]{0,1:T(8,128)(2,1)}) %all-gather.6.cloned.1.call-update) | async-done | bytes 2359312 | tf_op jit(solution)/shard_map/all_gather | solution.py:46
  185.7 0.0 copy-done.3
  185.7 4.6 %fusion.25 = (f32[]{:T(128)}, bf16[256,512]{1,0:T(8,128)(2,1)S(1)}) fusion(s32[2,128,512]{2,1,0:T(8,128)S(1)} %copy-done.3, f32[512]{0:T(512)S(1)} %add.86, bf16[1536,512]{0,1:T(8,128)(2,1)} %all-gather.8.cloned.1.call-done, bf16[768,1536]{0,1:T(8,128)(2,1)} %all-gather.6.cloned.1.call-done, f32[256,768]{1,0:T(8,128)S(1)} %fusion.7, ...), kind=kOutput, calls=%fused_computation.40 | convolution fusion | flops 1012072448 | bytes 6293508 | tf_op jit(solution)/shard_map/dot_general | solution.py:21
  190.2 0.0 copy-done.6
  190.2 2.1 fusion.44
  192.4 0.0 copy-done.2
  192.4 0.2 copy-done.7
  192.6 1.1 fusion.15
  193.6 1.3 collective-permute-start.2
  194.9 5.5 %collective-permute-start.3 = (bf16[2,128,768]{2,1,0:T(8,128)(2,1)S(1)}, bf16[2,128,768]{2,1,0:T(8,128)(2,1)S(1)}, u32[]{:S(2)}, u32[]{:S(2)}) collective-permute-start(bf16[2,128,768]{2,1,0:T(8,128)(2,1)S(1)} %bitcast.63), channel_id=1, source_target_pairs={{0,8},{1,9},{2,10},{3,11},{4,12},{5,13},{6,14},{7,15},{16,24},{17,... | collective-permute-start | bytes 1179656 | tf_op jit(solution)/shard_map/ppermute | solution.py:12
  200.4 3.7 %fusion.1 = f32[256,1536]{1,0:T(8,128)} fusion(bf16[256,768]{1,0:T(8,128)(2,1)S(1)} %fusion.15, bf16[3,1536,768]{2,1,0:T(8,128)(2,1)} %all-gather.4.cloned.1.call-done), kind=kOutput, calls=%fused_computation.8 | convolution fusion | flops 603979776 | bytes 4325376 | tf_op jit(solution)/shard_map/dot_general | solution.py:35
  204.1 32.7 %psum.7 = f32[]{:T(128)} all-reduce(f32[]{:T(128)} %get-tuple-element.2), channel_id=1, replica_groups=mesh['grp'=2,'seq'=16] {'seq'}, use_global_device_ids=true, to_apply=%region_3.4 | all-reduce | flops 1 | bytes 8 | tf_op jit(solution)/shard_map/psum | solution.py:68
  237.4 0.0 collective-permute-done.2
  237.5 2.9 %convolution_add_fusion.1 = f32[256,1536]{1,0:T(8,128)S(1)} fusion(f32[256,1536]{1,0:T(8,128)} %fusion.1, bf16[256,768]{1,0:T(8,128)(2,1)S(1)} %bitcast.59, bf16[3,1536,768]{2,1,0:T(8,128)(2,1)} %all-gather.4.cloned.1.call-done), kind=kOutput, calls=%fused_computation.1 | convolution fusion | flops 604372992 | bytes 5898240 | tf_op jit(solution)/shard_map/dot_general | solution.py:35
  240.4 0.0 collective-permute-done.3
  240.4 0.0 copy-start.1
  240.4 2.5 convolution_add_fusion
  243.0 0.0 copy-done.1
  243.0 0.3 multiply_reduce_fusion
  243.3 1.3 fusion.6
  (6 shorter events, 0.0 us)
Async XLA Ops:
  7.2 11.9 %copy-start.5 = (u32[32]{0:T(128)S(1)}, u32[32]{0:T(128)}, u32[]{:S(2)}) copy-start(u32[32]{0:T(128)} %constant.32) | copy-start | bytes 388
  7.2 3.6 %copy-start = (bf16[2,128,1536]{2,1,0:T(8,128)(2,1)S(1)}, bf16[2,128,1536]{2,1,0:T(8,128)(2,1)}, u32[]{:S(2)}) copy-start(bf16[2,128,1536]{2,1,0:T(8,128)(2,1)} %param.7) | copy-start | bytes 2359300
  7.2 13.2 %copy-start.4 = (bf16[1,32]{1,0:T(2,128)(2,1)S(1)}, bf16[1,32]{1,0:T(2,128)(2,1)}, u32[]{:S(2)}) copy-start(bf16[1,32]{1,0:T(2,128)(2,1)} %param.12) | copy-start | bytes 196
  7.2 94.7 %all-gather.4.cloned.1.call-start = ((), (), s32[]{:S(2)}) async-start(), calls=%async_computation | async-start | bytes 7520256 | tf_op jit(solution)/shard_map/all_gather | solution.py:45
  7.9 134.4 %all-gather.8.cloned.1.call-start = ((), (), s32[]{:S(2)}) async-start(), calls=%async_computation.2 | async-start | bytes 1671168 | tf_op jit(solution)/shard_map/all_gather | solution.py:64
  8.7 177.0 %all-gather.6.cloned.1.call-start = ((), (), s32[]{:S(2)}) async-start(), calls=%async_computation.1 | async-start | bytes 2506752 | tf_op jit(solution)/shard_map/all_gather | solution.py:46
  11.7 92.6 %collective-permute-start = (bf16[2,128,1536]{2,1,0:T(8,128)(2,1)S(1)}, bf16[2,128,1536]{2,1,0:T(8,128)(2,1)S(1)}, u32[]{:S(2)}, u32[]{:S(2)}) collective-permute-start(bf16[2,128,1536]{2,1,0:T(8,128)(2,1)S(1)} %multiply_convert_fusion), channel_id=1, source_target_pairs={{0,8},{1,9},{2,10},{3,11},{4,12},{5,13},{6,14},{7,15},{16,24},{17,... | collective-permute-start | bytes 2359304 | tf_op jit(solution)/shard_map/ppermute | solution.py:12
  17.8 89.1 %collective-permute-start.1 = (bf16[2,128,1536]{2,1,0:T(8,128)(2,1)S(1)}, bf16[2,128,1536]{2,1,0:T(8,128)(2,1)S(1)}, u32[]{:S(2)}, u32[]{:S(2)}) collective-permute-start(bf16[2,128,1536]{2,1,0:T(8,128)(2,1)S(1)} %multiply_convert_fusion), channel_id=1, source_target_pairs={{8,0},{9,1},{10,2},{11,3},{12,4},{13,5},{14,6},{15,7},{24,16},{25,... | collective-permute-start | bytes 2359304 | tf_op jit(solution)/shard_map/ppermute | solution.py:12
  106.8 78.8 %copy-start.3 = (s32[2,128,512]{2,1,0:T(8,128)S(1)}, s32[2,128,512]{2,1,0:T(8,128)}, u32[]{:S(2)}) copy-start(s32[2,128,512]{2,1,0:T(8,128)} %param.13) | copy-start | bytes 1572868
  109.4 80.9 %copy-start.6 = (f32[256,768]{1,0:T(8,128)}, f32[256,768]{1,0:T(8,128)S(1)}, u32[]{:S(2)}) copy-start(f32[256,768]{1,0:T(8,128)S(1)} %fusion.7) | copy-start | bytes 2359300
  190.2 2.1 copy-start.2
  190.2 2.3 copy-start.7
  193.6 43.8 %collective-permute-start.2 = (bf16[2,128,768]{2,1,0:T(8,128)(2,1)S(1)}, bf16[2,128,768]{2,1,0:T(8,128)(2,1)S(1)}, u32[]{:S(2)}, u32[]{:S(2)}) collective-permute-start(bf16[2,128,768]{2,1,0:T(8,128)(2,1)S(1)} %bitcast.62), channel_id=1, source_target_pairs={{8,0},{9,1},{10,2},{11,3},{12,4},{13,5},{14,6},{15,7},{24,16},{25,... | collective-permute-start | bytes 1179656 | tf_op jit(solution)/shard_map/ppermute | solution.py:12
  194.9 45.5 %collective-permute-start.3 = (bf16[2,128,768]{2,1,0:T(8,128)(2,1)S(1)}, bf16[2,128,768]{2,1,0:T(8,128)(2,1)S(1)}, u32[]{:S(2)}, u32[]{:S(2)}) collective-permute-start(bf16[2,128,768]{2,1,0:T(8,128)(2,1)S(1)} %bitcast.63), channel_id=1, source_target_pairs={{0,8},{1,9},{2,10},{3,11},{4,12},{5,13},{6,14},{7,15},{16,24},{17,... | collective-permute-start | bytes 1179656 | tf_op jit(solution)/shard_map/ppermute | solution.py:12
  240.4 2.5 %copy-start.1 = (f32[1536]{0:T(1024)S(1)}, f32[1536]{0:T(1024)}, u32[]{:S(2)}) copy-start(f32[1536]{0:T(1024)} %param.8) | copy-start | bytes 18436
Sparse Core Ops, SparseCore 0:
  10.3 91.5 all-gather.3
  104.2 38.0 all-gather.7
  144.6 41.0 all-gather.5
where the time goes:
time: 253 us; the launch traced here: 252 us
  waiting for transfers between devices  110 us (43%)
  blocking collectives  82.7 us (33%)
  matrix products  24.3 us (10%)
  between operations  16.4 us (6%)
  starting transfers between devices  14.2 us (6%)
  other arithmetic  4.01 us (2%)
    unnamed x1, blocking collectives  50.1 us
    all_gather x1, waiting for transfers between devices, shards(): lax.all_gather(proj_weight, 'seq', axis=1, tiled=True)  43.3 us
    all_gather x1, waiting for transfers between devices, shards(): lax.all_gather(head_weight, 'seq', axis=1, tiled=True)  33 us
    psum x1, blocking collectives, shards(): summed_loss = lax.psum(loss_total, 'seq')  32.7 us
    all_gather x1, waiting for transfers between devices, shards(): lax.all_gather(conv_weight, 'seq', axis=1, tiled=True)  31.3 us
    ppermute x4, starting transfers between devices, shifted(): lax.ppermute(value, axis, [(source, source + steps) for source in range(i...  14.1 us
    dot_general x4, matrix products, back_dot(): lax.dot_general(left, right, (((1,), (1,)), ((), ())), preferred_element_...  10.2 us
  transfers between devices with their start and end apart: 7, of which 3 were waited for; matrix products, arithmetic and copies ran while one was open for 7% of the time, Pallas kernels for 0%

commit v1 on v0

--- a/solution.py
+++ b/solution.py
@@ -43,7 +43,9 @@
     track_count = counts.shape[2]
     conv_full, proj_full = (
         lax.all_gather(conv_weight, "seq", axis=1, tiled=True),
-        lax.all_gather(proj_weight, "seq", axis=1, tiled=True),
+        jnp.concatenate(
+            lax.all_to_all(jnp.stack([proj_weight] * lax.axis_size("seq")), "seq", 0, 0), axis=1
+        ),
     )
     inner = conv_full.shape[2]
     inputs_f = inputs.astype(jnp.float32)

time: 253 us -> 245 us (0.968)
  waiting for transfers between devices: 110 us -> 41.5 us
  blocking collectives: 82.7 us -> 132 us
  starting transfers between devices: 14.2 us -> 21.3 us
  local copies, waits for them, and re-layouts: 1.05 us -> 3.63 us
    unnamed x1, blocking collectives: 50.1 us -> 99.7 us
    all_gather x1 -> x0, waiting for transfers between devices: 43.3 us -> none  [shards(): lax.all_gather(proj_weight, 'seq', axis=1, tiled=True)]
    all_gather x1, waiting for transfers between devices: 31.3 us -> 8.27 us  [shards(): lax.all_gather(conv_weight, 'seq', axis=1, tiled=True)]
    all_gather x1, waiting for transfers between devices: 33 us -> 24.6 us  [shards(): lax.all_gather(head_weight, 'seq', axis=1, tiled=True)]
    all_to_all x0 -> x1, starting transfers between devices: none -> 7.52 us  [shards(): lax.all_to_all(jnp.stack([proj_weight] * lax.axis_size('seq')), 'seq', 0, 0)]
    ppermute x4, waiting for transfers between devices: 0.01 us -> 7.17 us  [shifted(): lax.ppermute(value, axis, [(source, source + steps) for source in range(i...]
    another operation x0 -> x1, local copies, waits for them, and re-layouts: none -> 2.6 us  [shards(): jnp.stack([proj_weight] * lax.axis_size('seq'))]
  transfers between devices with their start and end apart: 7 -> 7, of which waited for: 3 -> 3; matrix products, arithmetic and copies ran while one was open for 7% -> 8% of each run, Pallas kernels for 0% -> 0%
where the time goes in v1:
time: 245 us
  blocking collectives  132 us (54%)
  waiting for transfers between devices  41.5 us (17%)
  matrix products  26.3 us (11%)
  starting transfers between devices  21.3 us (9%)
  between operations  16.6 us (7%)
  local copies, waits for them, and re-layouts  3.63 us (1%)
  other arithmetic  3.05 us (1%)
    unnamed x1, blocking collectives  99.7 us
    psum x1, blocking collectives, shards(): summed_loss = lax.psum(loss_total, 'seq')  32.7 us
    all_gather x1, waiting for transfers between devices, shards(): lax.all_gather(head_weight, 'seq', axis=1, tiled=True)  24.6 us
    ppermute x4, starting transfers between devices, shifted(): lax.ppermute(value, axis, [(source, source + steps) for source in range(i...  13.7 us
    dot_general x4, matrix products, back_dot(): lax.dot_general(left, right, (((1,), (1,)), ((), ())), preferred_element_...  10.2 us
    all_gather x1, waiting for transfers between devices, shards(): lax.all_gather(conv_weight, 'seq', axis=1, tiled=True)  8.27 us
    all_to_all x1, starting transfers between devices, shards(): lax.all_to_all(jnp.stack([proj_weight] * lax.axis_size('seq')), 'seq', 0, 0)  7.52 us
    ppermute x4, waiting for transfers between devices, shifted(): lax.ppermute(value, axis, [(source, source + steps) for source in range(i...  7.17 us
  transfers between devices with their start and end apart: 7, of which 3 were waited for; matrix products, arithmetic and copies ran while one was open for 8% of the time, Pallas kernels for 0%

profile of v1, /device:TPU:0, one launch (start us, length us, event | category | flops | bytes accessed | tf_op | source)
XLA Modules:
  0.0 244.8 jit_solution(18380090636796836960)
XLA Ops:
  7.2 0.0 all-gather.3.cloned.1.call-start
  7.2 0.7 all-gather.3.cloned.1.call-update
  7.9 2.6 %stack.2 = bf16[16,768,96]{1,2,0:T(8,128)(2,1)} broadcast(bf16[768,96]{0,1:T(8,128)(2,1)} %param.10), dimensions={1,2} | broadcast | bytes 2506752 | tf_op jit(solution)/shard_map/stack | solution.py:47
  10.5 0.0 copy-start
  10.5 0.0 copy-start.3
  10.5 7.5 %all-to-all-start = ((bf16[16,768,96]{1,2,0:T(8,128)(2,1)}), bf16[16,768,96]{1,2,0:T(8,128)(2,1)S(1)}, u32[]{:S(2)}, u32[]{:S(2)}) async-start(bf16[16,768,96]{1,2,0:T(8,128)(2,1)} %stack.2), calls=%async_computation | async-start | bytes 4718592 | tf_op jit(solution)/shard_map/all_to_all | solution.py:47
  18.0 0.0 copy-start.5
  18.0 0.0 copy-start.4
  18.0 0.0 all-gather.5.cloned.1.call-start
  18.1 0.7 all-gather.5.cloned.1.call-update
  18.8 0.0 copy-done
  18.8 0.2 multiply_reduce_fusion.1
  19.1 0.0 copy-done.3
  19.1 1.1 multiply_convert_fusion
  20.2 5.6 %collective-permute-start = (bf16[2,128,1536]{2,1,0:T(8,128)(2,1)}, bf16[2,128,1536]{2,1,0:T(8,128)(2,1)}, u32[]{:S(2)}, u32[]{:S(2)}) collective-permute-start(bf16[2,128,1536]{2,1,0:T(8,128)(2,1)} %multiply_convert_fusion), channel_id=1, source_target_pairs={{0,8},{1,9},{2,10},{3,11},{4,12},{5,13},{6,14},{7,15},{16,24},{17,... | collective-permute-start | bytes 2359304 | tf_op jit(solution)/shard_map/ppermute | solution.py:12
  25.8 1.3 collective-permute-start.1
  27.1 0.0 copy-done.5
  27.1 0.6 dynamic-slice
  28.3 0.0 copy-done.4
  28.4 0.2 dynamic-update-slice
  28.6 99.7 %all-reduce = bf16[512]{0:T(512)(128)(2,1)S(1)} all-reduce(bf16[512]{0:T(512)(128)(2,1)S(1)} %dynamic-update-slice), channel_id=1, replica_groups=mesh['grp'=2,'seq'=16] {'seq'}, use_global_device_ids=true, to_apply=%add | all-reduce | flops 512 | bytes 2048
  128.3 8.3 %all-gather.3.cloned.1.call-done = bf16[3,1536,768]{2,1,0:T(8,128)(2,1)} async-done(((bf16[3,96,768]{2,1,0:T(8,128)(2,1)}), bf16[3,1536,768]{2,1,0:T(8,128)(2,1)}) %all-gather.3.cloned.1.call-update) | async-done | bytes 7077904 | tf_op jit(solution)/shard_map/all_gather | solution.py:45
  136.6 2.7 %fusion.2 = f32[256,768]{1,0:T(8,128)S(1)} fusion(bf16[256,1536]{1,0:T(8,128)(2,1)} %bitcast.2, bf16[3,1536,768]{2,1,0:T(8,128)(2,1)} %all-gather.3.cloned.1.call-done), kind=kOutput, calls=%fused_computation.9 | convolution fusion | flops 603979776 | bytes 3932160 | tf_op jit(solution)/shard_map/dot_general | solution.py:56
  139.3 0.0 collective-permute-done
  139.3 2.7 %fusion.8 = f32[256,768]{1,0:T(8,128)S(1)} fusion(f32[256,768]{1,0:T(8,128)S(1)} %fusion.2, bf16[256,1536]{1,0:T(8,128)(2,1)} %bitcast.4, bf16[3,1536,768]{2,1,0:T(8,128)(2,1)} %all-gather.3.cloned.1.call-done), kind=kOutput, calls=%fused_computation.19 | convolution fusion | flops 604176384 | bytes 4718592 | tf_op jit(solution)/shard_map/dot_general | solution.py:57
  142.0 7.2 %collective-permute-done.1 = bf16[2,128,1536]{2,1,0:T(8,128)(2,1)} collective-permute-done((bf16[2,128,1536]{2,1,0:T(8,128)(2,1)}, bf16[2,128,1536]{2,1,0:T(8,128)(2,1)}, u32[]{:S(2)}, u32[]{:S(2)}) %collective-permute-start.1) | collective-permute-done | bytes 786464 | tf_op jit(solution)/shard_map/ppermute | solution.py:12
  149.2 3.6 %fusion.7 = f32[256,768]{1,0:T(8,128)} fusion(f32[256,768]{1,0:T(8,128)S(1)} %fusion.8, bf16[256,1536]{1,0:T(8,128)(2,1)} %bitcast.6, bf16[3,1536,768]{2,1,0:T(8,128)(2,1)} %all-gather.3.cloned.1.call-done), kind=kOutput, calls=%fused_computation.18 | convolution fusion | flops 604176384 | bytes 4718592 | tf_op jit(solution)/shard_map/dot_general | solution.py:58
  152.8 24.6 %all-gather.5.cloned.1.call-done = bf16[1536,512]{0,1:T(8,128)(2,1)} async-done(((bf16[1536,32]{0,1:T(8,128)(2,1)}), bf16[1536,512]{0,1:T(8,128)(2,1)}) %all-gather.5.cloned.1.call-update) | async-done | bytes 1572880 | tf_op jit(solution)/shard_map/all_gather | solution.py:66
  177.4 0.0 all-to-all-done
  177.4 0.0 copy-start.1
  177.4 5.0 %fusion.25 = (f32[]{:T(128)}, bf16[256,512]{1,0:T(8,128)(2,1)S(1)}) fusion(s32[2,128,512]{2,1,0:T(8,128)} %param.13, f32[512]{0:T(512)S(1)} %add.86, bf16[1536,512]{0,1:T(8,128)(2,1)} %all-gather.5.cloned.1.call-done, bf16[768,1536]{0,1:T(8,128)(2,1)S(1)} %bitcast.60, f32[256,768]{1,0:T(8,128)} %fusion.7, bf16[256,1536]{1,0:T(8,128)(2,1)S(1)} %bitcast.58), kind=kOutput, calls=%fused_computation.40 | convolution fusion | flops 1012072448 | bytes 6293508 | tf_op jit(solution)/shard_map/dot_general | solution.py:21
  182.4 0.0 copy-done.1
  182.4 0.0 copy-start.2
  182.4 0.0 copy-start.6
  182.4 2.1 fusion.44
  184.6 0.0 copy-done.2
  184.6 0.2 copy-done.6
  184.8 1.1 fusion.15
  185.8 1.3 collective-permute-start.2
  187.1 5.5 %collective-permute-start.3 = (bf16[2,128,768]{2,1,0:T(8,128)(2,1)S(1)}, bf16[2,128,768]{2,1,0:T(8,128)(2,1)S(1)}, u32[]{:S(2)}, u32[]{:S(2)}) collective-permute-start(bf16[2,128,768]{2,1,0:T(8,128)(2,1)S(1)} %bitcast.65), channel_id=1, source_target_pairs={{0,8},{1,9},{2,10},{3,11},{4,12},{5,13},{6,14},{7,15},{16,24},{17,... | collective-permute-start | bytes 1179656 | tf_op jit(solution)/shard_map/ppermute | solution.py:12
  192.6 3.7 %fusion.1 = f32[256,1536]{1,0:T(8,128)} fusion(bf16[256,768]{1,0:T(8,128)(2,1)S(1)} %fusion.15, bf16[3,1536,768]{2,1,0:T(8,128)(2,1)} %all-gather.3.cloned.1.call-done), kind=kOutput, calls=%fused_computation.8 | convolution fusion | flops 603979776 | bytes 4325376 | tf_op jit(solution)/shard_map/dot_general | solution.py:35
  196.3 32.7 %psum.7 = f32[]{:T(128)} all-reduce(f32[]{:T(128)} %get-tuple-element.2), channel_id=1, replica_groups=mesh['grp'=2,'seq'=16] {'seq'}, use_global_device_ids=true, to_apply=%region_3.4 | all-reduce | flops 1 | bytes 8 | tf_op jit(solution)/shard_map/psum | solution.py:70
  229.6 0.0 collective-permute-done.2
  229.6 2.9 %convolution_add_fusion.1 = f32[256,1536]{1,0:T(8,128)S(1)} fusion(f32[256,1536]{1,0:T(8,128)} %fusion.1, bf16[256,768]{1,0:T(8,128)(2,1)S(1)} %bitcast.63, bf16[3,1536,768]{2,1,0:T(8,128)(2,1)} %all-gather.3.cloned.1.call-done), kind=kOutput, calls=%fused_computation.1 | convolution fusion | flops 604372992 | bytes 5898240 | tf_op jit(solution)/shard_map/dot_general | solution.py:35
  232.6 0.0 collective-permute-done.3
  232.6 2.5 %convolution_add_fusion = f32[256,1536]{1,0:T(8,128)S(1)} fusion(f32[256,1536]{1,0:T(8,128)S(1)} %convolution_add_fusion.1, bf16[256,768]{1,0:T(8,128)(2,1)S(1)} %bitcast.62, bf16[3,1536,768]{2,1,0:T(8,128)(2,1)} %all-gather.3.cloned.1.call-done), kind=kOutput, calls=%fused_computation | convolution fusion | flops 604372992 | bytes 5898240 | tf_op jit(solution)/shard_map/dot_general | solution.py:35
  235.1 0.3 multiply_reduce_fusion
  235.4 1.3 fusion.6
  (4 shorter events, 0.0 us)
Async XLA Ops:
  7.2 129.5 %all-gather.3.cloned.1.call-start = ((), (), s32[]{:S(2)}) async-start(), calls=%async_computation.1 | async-start | bytes 7520256 | tf_op jit(solution)/shard_map/all_gather | solution.py:45
  10.5 8.3 %copy-start = (bf16[2,128,1536]{2,1,0:T(8,128)(2,1)S(1)}, bf16[2,128,1536]{2,1,0:T(8,128)(2,1)}, u32[]{:S(2)}) copy-start(bf16[2,128,1536]{2,1,0:T(8,128)(2,1)} %param.7) | copy-start | bytes 2359300
  10.5 8.6 %copy-start.3 = (f32[1536]{0:T(1024)S(1)}, f32[1536]{0:T(1024)}, u32[]{:S(2)}) copy-start(f32[1536]{0:T(1024)} %param.8) | copy-start | bytes 18436
  10.5 166.9 %all-to-all-start = ((bf16[16,768,96]{1,2,0:T(8,128)(2,1)}), bf16[16,768,96]{1,2,0:T(8,128)(2,1)S(1)}, u32[]{:S(2)}, u32[]{:S(2)}) async-start(bf16[16,768,96]{1,2,0:T(8,128)(2,1)} %stack.2), calls=%async_computation | async-start | bytes 4718592 | tf_op jit(solution)/shard_map/all_to_all | solution.py:47
  18.0 9.1 %copy-start.5 = (u32[32]{0:T(128)S(1)}, u32[32]{0:T(128)}, u32[]{:S(2)}) copy-start(u32[32]{0:T(128)} %constant.32) | copy-start | bytes 388
  18.0 10.3 %copy-start.4 = (bf16[1,32]{1,0:T(2,128)(2,1)S(1)}, bf16[1,32]{1,0:T(2,128)(2,1)}, u32[]{:S(2)}) copy-start(bf16[1,32]{1,0:T(2,128)(2,1)} %param.12) | copy-start | bytes 196
  18.0 159.4 %all-gather.5.cloned.1.call-start = ((), (), s32[]{:S(2)}) async-start(), calls=%async_computation.2 | async-start | bytes 1671168 | tf_op jit(solution)/shard_map/all_gather | solution.py:66
  20.2 119.1 %collective-permute-start = (bf16[2,128,1536]{2,1,0:T(8,128)(2,1)}, bf16[2,128,1536]{2,1,0:T(8,128)(2,1)}, u32[]{:S(2)}, u32[]{:S(2)}) collective-permute-start(bf16[2,128,1536]{2,1,0:T(8,128)(2,1)} %multiply_convert_fusion), channel_id=1, source_target_pairs={{0,8},{1,9},{2,10},{3,11},{4,12},{5,13},{6,14},{7,15},{16,24},{17,... | collective-permute-start | bytes 2359304 | tf_op jit(solution)/shard_map/ppermute | solution.py:12
  25.8 123.4 %collective-permute-start.1 = (bf16[2,128,1536]{2,1,0:T(8,128)(2,1)}, bf16[2,128,1536]{2,1,0:T(8,128)(2,1)}, u32[]{:S(2)}, u32[]{:S(2)}) collective-permute-start(bf16[2,128,1536]{2,1,0:T(8,128)(2,1)} %multiply_convert_fusion), channel_id=1, source_target_pairs={{8,0},{9,1},{10,2},{11,3},{12,4},{13,5},{14,6},{15,7},{24,16},{25,... | collective-permute-start | bytes 2359304 | tf_op jit(solution)/shard_map/ppermute | solution.py:12
  177.4 5.0 %copy-start.1 = (bf16[16,768,96]{1,2,0:T(8,128)(2,1)}, bf16[16,768,96]{1,2,0:T(8,128)(2,1)S(1)}, u32[]{:S(2)}) copy-start(bf16[16,768,96]{1,2,0:T(8,128)(2,1)S(1)} %all-to-all-done) | copy-start | bytes 7077892
  182.4 2.1 copy-start.2
  182.4 2.3 copy-start.6
  185.8 43.8 %collective-permute-start.2 = (bf16[2,128,768]{2,1,0:T(8,128)(2,1)S(1)}, bf16[2,128,768]{2,1,0:T(8,128)(2,1)S(1)}, u32[]{:S(2)}, u32[]{:S(2)}) collective-permute-start(bf16[2,128,768]{2,1,0:T(8,128)(2,1)S(1)} %bitcast.64), channel_id=1, source_target_pairs={{8,0},{9,1},{10,2},{11,3},{12,4},{13,5},{14,6},{15,7},{24,16},{25,... | collective-permute-start | bytes 1179656 | tf_op jit(solution)/shard_map/ppermute | solution.py:12
  187.1 45.4 %collective-permute-start.3 = (bf16[2,128,768]{2,1,0:T(8,128)(2,1)S(1)}, bf16[2,128,768]{2,1,0:T(8,128)(2,1)S(1)}, u32[]{:S(2)}, u32[]{:S(2)}) collective-permute-start(bf16[2,128,768]{2,1,0:T(8,128)(2,1)S(1)} %bitcast.65), channel_id=1, source_target_pairs={{0,8},{1,9},{2,10},{3,11},{4,12},{5,13},{6,14},{7,15},{16,24},{17,... | collective-permute-start | bytes 1179656 | tf_op jit(solution)/shard_map/ppermute | solution.py:12
Sparse Core Ops, SparseCore 0:
  10.3 126.3 all-gather.2
  138.9 38.4 all-gather.4
